TPU v7x, 32 devices: a whole 2x2x4 slice. The times are simulated.
32 devices in a mesh: grp: 2 (over x), seq: 16 (over z, y, core).
Axes of the slice: x: 2, y: 2, z: 4, core: 2. Of those that a mesh axis runs over, the one named last changes fastest.
Arguments:
- hidden: bfloat16 [16384, 4096], P(('grp', 'seq')), parts along dimension 0, may hold values from -6 to 6
- token_ids: int32 [32, 512], P(('grp', 'seq')), parts along dimension 0, may hold values from 0 to 128255, as said below
- upstream: bfloat16 [16384, 1024], P(('grp', 'seq')), parts along dimension 0, may hold values from -6 to 6
- w_value: bfloat16 [4096, 1024], P('seq'), may hold values from -0.09375 to 0.09375
- proj_in: bfloat16 [4096, 64], replicated, may hold values from -0.09375 to 0.09375
- proj_out: bfloat16 [8, 128, 64], replicated, may hold values from -0.5 to 0.5
- in_inverse: float32 [8, 64, 64], replicated
- out_inverse: float32 [8, 64, 64], replicated
- datastore: bfloat16 [1024, 32768], P(('grp', 'seq')), parts along dimension 0
Outputs:
- input_grad: bfloat16 [16384, 4096], P(('grp', 'seq')), parts along dimension 0
- scores: float32 [32, 512], P('grp', 'seq'), parts along dimension 0
There are 2 independent parts, one for each index of `grp`. A program takes and returns all parts, laid end to end along the dimension named above; an argument that names none is the same for every part. Nothing has to cross between parts.
Inputs may be any that keep to these rules, and one draw needn't show every extreme that they name: `token_ids`: each sequence holds its live tokens first, then padding ids 0; at least 128 tokens of every sequence are live and some sequence has no padding.
All inputs are finite; a program needn't handle non-finite values.
Results may differ from a plain program's by a relative error of at most 0.0059.
Values may be sent and summed in bfloat16 or wider, within the bound.
A program may use at most 128 MiB of HBM per device.

v0:
```python
import jax
import jax.numpy as jnp
from jax import lax
from jax.sharding import PartitionSpec as P

KVH = 8
HD = 128
RANK = 64


def on_device(
    hidden, token_ids, upstream, w_value, proj_in, proj_out, in_inverse, out_inverse, datastore
):
    local_queries = token_ids.shape[0]
    seq_tokens = token_ids.shape[1]
    live_mask = (token_ids != 0).reshape(-1, 1).astype(jnp.bfloat16)
    masked = upstream * live_mask
    contract_last = (((1,), (1,)), ((), ()))
    full_weight = lax.all_gather(w_value, "seq", axis=0, tiled=True)
    input_grad = lax.dot_general(
        masked, full_weight, contract_last, preferred_element_type=jnp.float32
    ).astype(jnp.bfloat16)
    left_proj = jnp.dot(hidden, proj_in, preferred_element_type=jnp.float32).astype(jnp.bfloat16)
    cot_heads = masked.reshape(-1, KVH, HD)
    right_proj = jnp.einsum(
        "thd,hdr->thr", cot_heads, proj_out, preferred_element_type=jnp.float32
    ).astype(jnp.bfloat16)
    left_seq = left_proj.reshape(local_queries, seq_tokens, RANK)
    right_seq = right_proj.reshape(local_queries, seq_tokens, KVH, RANK)
    raw_grads = jnp.einsum(
        "qti,qthj->qhij", left_seq, right_seq, preferred_element_type=jnp.float32
    )
    half_way = jnp.einsum("hai,qhij->qhaj", in_inverse, raw_grads, precision=lax.Precision.HIGHEST)
    pre_grads = jnp.einsum("qhaj,hjb->qhab", half_way, out_inverse, precision=lax.Precision.HIGHEST)
    query_grads = pre_grads.astype(jnp.bfloat16).reshape(local_queries, -1)
    raw_scores = lax.dot_general(
        lax.all_gather(query_grads, "seq", axis=0, tiled=True),
        datastore,
        contract_last,
        preferred_element_type=jnp.float32,
    )
    power_local = jnp.sum(raw_scores * raw_scores, axis=1)
    power_sum = lax.psum(power_local, "seq")
    row_total = datastore.shape[0] * lax.axis_size("seq")
    spread = jnp.sqrt(power_sum / row_total + 1e-06)
    return (input_grad, raw_scores / spread[:, None])


def solution(mesh):
    placed = (
        P(("grp", "seq"), None),
        P(("grp", "seq"), None),
        P(("grp", "seq"), None),
        P("seq", None),
        P(),
        P(),
        P(),
        P(),
        P(("grp", "seq"), None),
    )
    return jax.shard_map(
        on_device,
        mesh=mesh,
        in_specs=placed,
        out_specs=(P(("grp", "seq"), None), P("grp", "seq")),
        check_vma=False,
    )
```

profile of v0, /device:TPU:0, one launch (start us, length us, event | category | flops | bytes accessed | tf_op | source)
XLA Modules:
  0.0 152.7 jit_solution(1100063933830969309)
XLA Ops:
  7.2 0.0 copy-start
  7.2 0.0 copy-start.3
  7.2 0.0 copy-start.1
  7.2 0.0 copy-start.2
  7.2 0.0 all-gather.6.cloned.1.call-start
  7.3 0.9 fusion.14
  8.1 3.7 %fusion.4 = bf16[512,64,1]{0,1,2:T(8,128)(2,1)S(1)} fusion(bf16[512,4096]{1,0:T(8,128)(2,1)} %param.9, bf16[4096,64]{0,1:T(8,128)(2,1)} %param.13), kind=kOutput, calls=%fused_computation.9 | convolution fusion | flops 268468224 | bytes 4784128 | tf_op jit(solution)/shard_map/dot_general | solution.py:23
  11.8 0.0 copy-done.3
  11.8 2.0 %fusion.2 = f32[8,64,64]{1,2,0:T(8,128)S(1)} fusion(bf16[512,64,1]{0,1,2:T(8,128)(2,1)S(1)} %fusion.4, bf16[8,128,64]{1,2,0:T(8,128)(2,1)S(1)} %copy-done.3, bf16[512,1024]{1,0:T(8,128)(2,1)} %param.11, bf16[512]{0:T(512)(128)(2,1)S(1)} %fusion.14), kind=kOutput, calls=%fused_computation.5 | convolution fusion | flops 101449728 | bytes 1377280 | tf_op jit(solution)/shard_map/qti,qthj->qhij/dot_general | solution.py:30
  13.8 0.0 copy-done.1
  13.8 0.5 convolution_bitcast_fusion
  14.3 0.0 copy-done.2
  14.3 0.6 fusion.3
  15.0 0.8 reshape.42
  15.7 0.0 all-gather.6.cloned.1.call-update
  15.8 0.0 all-gather.4.cloned.1.call-start
  15.8 0.7 all-gather.4.cloned.1.call-update
  16.5 43.6 %all-gather.6.cloned.1.call-done = bf16[16,1,32768]{2,1,0:T(2,128)(2,1)} async-done(((bf16[1,1,32768]{2,1,0:T(2,128)(2,1)}), bf16[16,1,32768]{2,1,0:T(2,128)(2,1)}) %all-gather.6.cloned.1.call-update) | async-done | bytes 1048592 | tf_op jit(solution)/shard_map/all_gather | solution.py:37
  60.1 0.0 copy-done
  60.1 3.2 %multiply_reduce_fusion = (f32[16]{0:T(128)S(1)}, f32[16,32]{1,0:T(8,128)S(1)}) fusion(bf16[32,32768]{1,0:T(8,128)(2,1)S(1)} %copy-done, bf16[16,1,32768]{2,1,0:T(2,128)(2,1)} %all-gather.6.cloned.1.call-done), kind=kOutput, calls=%fused_computation.18 | convolution fusion | flops 33555440 | bytes 3147840 | tf_op jit(solution)/shard_map/dot_general | solution.py:36
  63.3 32.3 %psum.7 = f32[16]{0:T(128)S(1)} all-reduce(f32[16]{0:T(128)S(1)} %get-tuple-element.2), channel_id=1, replica_groups=mesh['grp'=2,'seq'=16] {'seq'}, use_global_device_ids=true, to_apply=%region_1.0 | all-reduce | flops 16 | bytes 128 | tf_op jit(solution)/shard_map/psum | solution.py:43
  95.6 0.7 broadcast_divide_fusion
  96.3 39.3 %all-gather.4.cloned.1.call-done = bf16[4096,1024]{1,0:T(8,128)(2,1)} async-done(((bf16[256,1024]{1,0:T(8,128)(2,1)}), bf16[4096,1024]{1,0:T(8,128)(2,1)}) %all-gather.4.cloned.1.call-update) | async-done | bytes 8388624 | tf_op jit(solution)/shard_map/all_gather | solution.py:19
  135.6 10.3 %convolution_convert_fusion = bf16[512,4096]{1,0:T(8,128)(2,1)} fusion(bf16[4096,1024]{1,0:T(8,128)(2,1)} %all-gather.4.cloned.1.call-done, bf16[512,1024]{1,0:T(8,128)(2,1)} %param.11, bf16[512]{0:T(512)(128)(2,1)S(1)} %fusion.14), kind=kOutput, calls=%fused_computation | convolution fusion | flops 4297588736 | bytes 13632512 | tf_op jit(solution)/shard_map/dot_general | solution.py:20
  (1 shorter events, 0.0 us)
Async XLA Ops:
  7.2 52.9 %copy-start = (bf16[32,32768]{1,0:T(8,128)(2,1)S(1)}, bf16[32,32768]{1,0:T(8,128)(2,1)}, u32[]{:S(2)}) copy-start(bf16[32,32768]{1,0:T(8,128)(2,1)} %param.17) | copy-start | bytes 6291460
  7.2 4.6 %copy-start.3 = (bf16[8,128,64]{1,2,0:T(8,128)(2,1)S(1)}, bf16[8,128,64]{1,2,0:T(8,128)(2,1)}, u32[]{:S(2)}) copy-start(bf16[8,128,64]{1,2,0:T(8,128)(2,1)} %param.14) | copy-start | bytes 393220
  7.2 6.6 %copy-start.1 = (f32[8,64,64]{2,1,0:T(8,128)S(1)}, f32[8,64,64]{2,1,0:T(8,128)}, u32[]{:S(2)}) copy-start(f32[8,64,64]{2,1,0:T(8,128)} %param.15) | copy-start | bytes 393220
  7.2 7.1 %copy-start.2 = (f32[8,64,64]{2,1,0:T(8,128)S(1)}, f32[8,64,64]{2,1,0:T(8,128)}, u32[]{:S(2)}) copy-start(f32[8,64,64]{2,1,0:T(8,128)} %param.16) | copy-start | bytes 393220
  7.2 52.9 %all-gather.6.cloned.1.call-start = ((), (), s32[]{:S(2)}) async-start(), calls=%async_computation.1 | async-start | bytes 2228224 | tf_op jit(solution)/shard_map/all_gather | solution.py:37
  15.8 119.8 %all-gather.4.cloned.1.call-start = ((), (), s32[]{:S(2)}) async-start(), calls=%async_computation | async-start | bytes 8912896 | tf_op jit(solution)/shard_map/all_gather | solution.py:19
Sparse Core Ops, SparseCore 0:
  15.9 44.1 all-gather.5
  62.3 73.2 all-gather.3
where the time goes:
time: 153 us
  waiting for transfers between devices  83.6 us (55%)
  blocking collectives  32.3 us (21%)
  matrix products  20.3 us (13%)
  between operations  14.1 us (9%)
  other arithmetic  1.55 us (1%)
    all_gather x1, waiting for transfers between devices, on_device(): lax.all_gather(query_grads, 'seq', axis=0, tiled=True)  43.6 us
    all_gather x1, waiting for transfers between devices, on_device(): full_weight = lax.all_gather(w_value, 'seq', axis=0, tiled=True)  39.3 us
    psum x1, blocking collectives, on_device(): power_sum = lax.psum(power_local, 'seq')  32.3 us
    dot_general x1, matrix products, on_device(): lax.dot_general(masked, full_weight, contract_last, preferred_element_typ...  10.3 us
    dot_general x1, matrix products, on_device(): jnp.dot(hidden, proj_in, preferred_element_type=jnp.float32)  3.69 us
    dot_general x1, matrix products, on_device(): lax.dot_general(lax.all_gather(query_grads, 'seq', axis=0, tiled=True), d...  3.16 us
  transfers between devices with their start and end apart: 2, of which 2 were waited for; matrix products, arithmetic and copies ran while one was open for 3% of the time, Pallas kernels for 0%

commit v1 on v0

--- a/solution.py
+++ b/solution.py
@@ -16,7 +16,9 @@
     live_mask = (token_ids != 0).reshape(-1, 1).astype(jnp.bfloat16)
     masked = upstream * live_mask
     contract_last = (((1,), (1,)), ((), ()))
-    full_weight = lax.all_gather(w_value, "seq", axis=0, tiled=True)
+    full_weight = jnp.concatenate(
+        lax.all_to_all(jnp.stack([w_value] * lax.axis_size("seq")), "seq", 0, 0), axis=0
+    )
     input_grad = lax.dot_general(
         masked, full_weight, contract_last, preferred_element_type=jnp.float32
     ).astype(jnp.bfloat16)

time: 153 us -> 250 us (1.63)
  the two profiles are of different devices: /device:TPU:0 before, /device:TPU:16 now
where the time goes in v1:
time: 250 us
  waiting for transfers between devices  130 us (52%)
  blocking collectives  71.9 us (29%)
  matrix products  20.2 us (8%)
  between operations  14.1 us (6%)
  starting transfers between devices  6.36 us (3%)
  local copies, waits for them, and re-layouts  6.3 us (3%)
    all_gather x1, waiting for transfers between devices, on_device(): lax.all_gather(query_grads, 'seq', axis=0, tiled=True)  130 us
    psum x1, blocking collectives, on_device(): power_sum = lax.psum(power_local, 'seq')  71.9 us
    dot_general x1, matrix products, on_device(): lax.dot_general(masked, full_weight, contract_last, preferred_element_typ...  10.3 us
    all_to_all x1, starting transfers between devices, on_device(): lax.all_to_all(jnp.stack([w_value] * lax.axis_size('seq')), 'seq', 0, 0)  6.32 us
    another operation x1, local copies, waits for them, and re-layouts, on_device(): jnp.stack([w_value] * lax.axis_size('seq'))  5.49 us
  transfers between devices with their start and end apart: 2, of which 1 were waited for; matrix products, arithmetic and copies ran while one was open for 5% of the time, Pallas kernels for 0%

profile of v1, /device:TPU:16, one launch (start us, length us, event | category | flops | bytes accessed | tf_op | source)
XLA Modules:
  0.0 250.1 jit_solution(6358649253408310359)
XLA Ops:
  7.2 0.0 copy-start
  7.2 5.5 %stack.2 = bf16[16,256,1024]{2,1,0:T(8,128)(2,1)} broadcast(bf16[256,1024]{1,0:T(8,128)(2,1)} %param.12), dimensions={1,2} | broadcast | bytes 8912896 | tf_op jit(solution)/shard_map/stack | solution.py:20
  12.7 0.0 copy-start.4
  12.7 0.0 copy-start.1
  12.7 6.3 %all-to-all-start = ((bf16[16,256,1024]{2,1,0:T(8,128)(2,1)}), bf16[16,256,1024]{2,1,0:T(8,128)(2,1)}, u32[]{:S(2)}, u32[]{:S(2)}) async-start(bf16[16,256,1024]{2,1,0:T(8,128)(2,1)} %stack.2), calls=%async_computation | async-start | bytes 16777216 | tf_op jit(solution)/shard_map/all_to_all | solution.py:20
  19.0 0.0 copy-start.5
  19.0 0.0 copy-start.2
  19.0 0.0 copy-start.3
  19.0 0.0 all-gather.3.cloned.1.call-start
  19.1 0.0 copy-done.4
  19.1 0.0 copy-done.1
  19.1 3.7 %fusion.4 = bf16[512,64,1]{0,1,2:T(8,128)(2,1)S(1)} fusion(bf16[512,4096]{1,0:T(8,128)(2,1)} %param.9, bf16[4096,64]{0,1:T(8,128)(2,1)S(1)} %copy-done.1), kind=kOutput, calls=%fused_computation.9 | convolution fusion | flops 268468224 | bytes 4784128 | tf_op jit(solution)/shard_map/dot_general | solution.py:25
  22.8 0.0 copy-done.5
  22.8 2.0 fusion.2
  24.8 0.0 copy-done.2
  24.8 0.5 convolution_bitcast_fusion
  25.3 0.0 copy-done.3
  25.3 0.6 fusion.3
  25.9 0.8 reshape.48
  26.7 0.0 all-gather.3.cloned.1.call-update
  26.7 130.4 %all-gather.3.cloned.1.call-done = bf16[16,1,32768]{2,1,0:T(2,128)(2,1)} async-done(((bf16[1,1,32768]{2,1,0:T(2,128)(2,1)}), bf16[16,1,32768]{2,1,0:T(2,128)(2,1)}) %all-gather.3.cloned.1.call-update) | async-done | bytes 1048592 | tf_op jit(solution)/shard_map/all_gather | solution.py:39
  157.2 0.0 copy-done
  157.2 3.2 %multiply_reduce_fusion = (f32[16]{0:T(128)S(1)}, f32[16,32]{1,0:T(8,128)S(1)}) fusion(bf16[32,32768]{1,0:T(8,128)(2,1)S(1)} %copy-done, bf16[16,1,32768]{2,1,0:T(2,128)(2,1)} %all-gather.3.cloned.1.call-done), kind=kOutput, calls=%fused_computation.18 | convolution fusion | flops 33555440 | bytes 3147840 | tf_op jit(solution)/shard_map/dot_general | solution.py:38
  160.3 71.9 %psum.7 = f32[16]{0:T(128)S(1)} all-reduce(f32[16]{0:T(128)S(1)} %get-tuple-element.2), channel_id=1, replica_groups=mesh['grp'=2,'seq'=16] {'seq'}, use_global_device_ids=true, to_apply=%region_1.0 | all-reduce | flops 16 | bytes 128 | tf_op jit(solution)/shard_map/psum | solution.py:45
  232.3 0.7 broadcast_divide_fusion
  233.0 0.0 all-to-all-done
  233.0 10.3 %convolution_convert_fusion = bf16[512,4096]{1,0:T(8,128)(2,1)} fusion(bf16[4096,1024]{1,0:T(8,128)(2,1)} %bitcast, bf16[512,1024]{1,0:T(8,128)(2,1)} %param.11, bf16[512]{0:T(512)(128)(2,1)S(1)} %fusion.14), kind=kOutput, calls=%fused_computation | convolution fusion | flops 4297588736 | bytes 13632512 | tf_op jit(solution)/shard_map/dot_general | solution.py:22
  (2 shorter events, 0.0 us)
Async XLA Ops:
  7.2 150.0 %copy-start = (bf16[32,32768]{1,0:T(8,128)(2,1)S(1)}, bf16[32,32768]{1,0:T(8,128)(2,1)}, u32[]{:S(2)}) copy-start(bf16[32,32768]{1,0:T(8,128)(2,1)} %param.17) | copy-start | bytes 6291460
  12.7 6.4 %copy-start.4 = (s32[1,512]{1,0:T(1,128)S(1)}, s32[1,512]{1,0:T(1,128)}, u32[]{:S(2)}) copy-start(s32[1,512]{1,0:T(1,128)} %param.10) | copy-start | bytes 6148
  12.7 6.4 %copy-start.1 = (bf16[4096,64]{0,1:T(8,128)(2,1)S(1)}, bf16[4096,64]{0,1:T(8,128)(2,1)}, u32[]{:S(2)}) copy-start(bf16[4096,64]{0,1:T(8,128)(2,1)} %param.13) | copy-start | bytes 1572868
  12.7 220.3 %all-to-all-start = ((bf16[16,256,1024]{2,1,0:T(8,128)(2,1)}), bf16[16,256,1024]{2,1,0:T(8,128)(2,1)}, u32[]{:S(2)}, u32[]{:S(2)}) async-start(bf16[16,256,1024]{2,1,0:T(8,128)(2,1)} %stack.2), calls=%async_computation | async-start | bytes 16777216 | tf_op jit(solution)/shard_map/all_to_all | solution.py:20
  19.0 3.8 %copy-start.5 = (bf16[8,128,64]{1,2,0:T(8,128)(2,1)S(1)}, bf16[8,128,64]{1,2,0:T(8,128)(2,1)}, u32[]{:S(2)}) copy-start(bf16[8,128,64]{1,2,0:T(8,128)(2,1)} %param.14) | copy-start | bytes 393220
  19.0 5.8 %copy-start.2 = (f32[8,64,64]{2,1,0:T(8,128)S(1)}, f32[8,64,64]{2,1,0:T(8,128)}, u32[]{:S(2)}) copy-start(f32[8,64,64]{2,1,0:T(8,128)} %param.15) | copy-start | bytes 393220
  19.0 6.3 %copy-start.3 = (f32[8,64,64]{2,1,0:T(8,128)S(1)}, f32[8,64,64]{2,1,0:T(8,128)}, u32[]{:S(2)}) copy-start(f32[8,64,64]{2,1,0:T(8,128)} %param.16) | copy-start | bytes 393220
  19.0 138.2 %all-gather.3.cloned.1.call-start = ((), (), s32[]{:S(2)}) async-start(), calls=%async_computation.1 | async-start | bytes 2228224 | tf_op jit(solution)/shard_map/all_gather | solution.py:39
Sparse Core Ops, SparseCore 0:
  26.9 130.2 all-gather.2
